TPU v7x, 256 devices: a whole 4x4x8 slice. The times are simulated.
256 devices in a mesh: blk: 128 (over y, z, x_lo, core), rhs: 2 (over x_hi).
Axes of the slice: x: 4 (x_hi: 2, x_lo: 2; x = x_hi * 2 + x_lo), y: 4, z: 8, core: 2. Of those that a mesh axis runs over, the one named last changes fastest.
Arguments:
- positions: float32 [3, 32768], P(None, 'blk'), may hold values from -1 to 1
- normal_angles: float32 [2, 32768], P(None, 'blk'), may hold values from -3.140625 to 3.140625
- areas: float32 [32768], P('blk'), may hold values from 1 to 6
- densities: float32 [2, 2, 32768], P('rhs', None, 'blk'), may hold values from -6 to 6
- need_owner: int32 [32768, 1], P('blk'), may hold values from 0 to 127; in each aligned block of 256 rows (0 to 255, 256 to 511, ...) at most 8 rows name the same one
- need_slot: int32 [32768], P('blk'), may hold values from 0 to 255
- near_index: int32 [32, 32768], P(None, 'blk'), may hold values from 0 to 255
- near_coef: float32 [2, 32, 32768], P(None, None, 'blk'), may hold values from -2 to 2
Outputs:
- result_field: float32 [2, 2, 32768], P('rhs', None, 'blk')
Inputs may be any that keep to these rules, and one draw needn't show every extreme that they name: `need_owner`: among the 256 entries of one block of targets, at most 8 name the same owner.
All inputs are finite; a program needn't handle non-finite values.
Results may differ from a plain program's by a relative error of at most 0.0003.
Values sent between devices are 32-bit elements; how exact they have to be, the bound alone decides.
A program may use at most 128 MiB of HBM per device.

v0:
```python
import math
import jax
import jax.numpy as jnp
from jax import lax
from jax.sharding import PartitionSpec as P

WAVE = 8.0
COUPLE = 1.0
SOFT = 0.1
TILE = 512


def unit_normals(angles):
    azimuth = angles[0]
    elevation = angles[1]
    return jnp.stack(
        [
            jnp.cos(azimuth) * jnp.cos(elevation),
            jnp.sin(azimuth) * jnp.cos(elevation),
            jnp.sin(elevation),
        ],
        0,
    )


def kernel_tile(targets, geometry):
    offset_vec = targets[:, :, None] - geometry[0:3, None, :]
    distance = jnp.sqrt(jnp.sum(offset_vec * offset_vec, 0) + SOFT * SOFT)
    facing = jnp.sum(offset_vec * geometry[3:6, None, :], 0)
    single = 1.0 / (4.0 * math.pi * distance)
    double = facing * single / (distance * distance)
    phases = WAVE * distance
    cosine = jnp.cos(phases)
    sines = jnp.sin(phases)
    weight = geometry[6][None, :]
    real_part = weight * (double * (cosine + phases * sines) + COUPLE * single * sines)
    imag_part = weight * (double * (sines - phases * cosine) - COUPLE * single * cosine)
    return (real_part, imag_part)


def apply_tile(targets, geometry, sources):
    real_part, imag_part = kernel_tile(targets, geometry)
    highest = lax.Precision.HIGHEST
    src_real = sources[:, 0, :]
    src_imag = sources[:, 1, :]
    out_real = jnp.einsum("ts,rs->rt", real_part, src_real, precision=highest) - jnp.einsum(
        "ts,rs->rt", imag_part, src_imag, precision=highest
    )
    out_imag = jnp.einsum("ts,rs->rt", real_part, src_imag, precision=highest) + jnp.einsum(
        "ts,rs->rt", imag_part, src_real, precision=highest
    )
    return (out_real, out_imag)


def far_block(running, targets, geometry, sources):
    more_real, more_imag = apply_tile(targets, geometry, sources)
    return (running[0] + more_real, running[1] + more_imag)


def far_piece(running, targets, geometry, flat_sources):
    count_rows = geometry.shape[1]
    side_count = flat_sources.shape[0] // 2
    sources = flat_sources.reshape(side_count, 2, count_rows)
    tile_width = math.gcd(count_rows, TILE)
    blocks = count_rows // tile_width
    geo_tiles = geometry.reshape(7, blocks, tile_width).transpose(1, 0, 2)
    src_tiles = sources.reshape(side_count, 2, blocks, tile_width).transpose(2, 0, 1, 3)

    def advance(partial_sums, tile_pair):
        return (far_block(partial_sums, targets, tile_pair[0], tile_pair[1]), None)

    running, _ = lax.scan(advance, running, (geo_tiles, src_tiles))
    return running


def near_field(needed, near_rows, near_terms):
    looked = needed[:, :, near_rows]
    coef_real = near_terms[0]
    coef_imag = near_terms[1]
    near_real = jnp.sum(coef_real * looked[:, 0] - coef_imag * looked[:, 1], 1)
    near_imag = jnp.sum(coef_real * looked[:, 1] + coef_imag * looked[:, 0], 1)
    return (near_real, near_imag)


def on_device(
    positions, normal_angles, areas, densities, need_owner, need_slot, near_index, near_coef
):
    own_rows = positions.shape[1]
    blk_count = lax.axis_size("blk")
    panels_all = own_rows * blk_count
    normals = unit_normals(normal_angles)
    weights = areas * (1.0 / math.sqrt(panels_all))
    geometry = jnp.concatenate([positions, normals, weights[None, :]], 0)
    owners = need_owner[:, 0]
    need_count = need_slot.shape[0]
    send_density = densities.reshape(2 * densities.shape[0], own_rows)
    side_count = send_density.shape[0] // 2
    target_count = positions.shape[1]
    empty_sum = jnp.zeros((side_count, target_count), jnp.float32)
    far_real, far_imag = far_piece(
        (empty_sum, empty_sum),
        positions,
        lax.all_gather(geometry, "blk", axis=1, tiled=True),
        lax.all_gather(send_density, "blk", axis=1, tiled=True),
    )
    near_sides = densities.shape[0]
    capacity = 4 * need_count // blk_count
    owner_ids = jnp.arange(blk_count, dtype=jnp.int32)
    onehot = (owners[:, None] == owner_ids[None, :]).astype(jnp.int32)
    before = jnp.cumsum(onehot, 0) - onehot
    ranks_in = jnp.sum(before * onehot, 1)
    placed = owners * capacity + ranks_in
    requests = (
        jnp.zeros((blk_count * capacity,), jnp.int32)
        .at[placed]
        .set(need_slot)
        .reshape(blk_count, capacity)
    )
    values = densities[
        :, :, lax.all_to_all(requests, "blk", split_axis=0, concat_axis=0, tiled=True)
    ]
    answers = lax.all_to_all(values, "blk", split_axis=2, concat_axis=2, tiled=True)
    needed = answers.reshape(near_sides, 2, blk_count * capacity)[:, :, placed]
    near_real, near_imag = near_field(needed, near_index, near_coef)
    far_real = far_real + near_real
    far_imag = far_imag + near_imag
    field_real = 0.5 * densities[:, 0] + far_real
    field_imag = 0.5 * densities[:, 1] + far_imag
    result_field = jnp.stack([field_real, field_imag], 1)
    return result_field


def solution(mesh):
    in_specs = (
        P(None, "blk"),
        P(None, "blk"),
        P("blk"),
        P("rhs", None, "blk"),
        P("blk", None),
        P("blk"),
        P(None, "blk"),
        P(None, None, "blk"),
    )
    out_specs = P("rhs", None, "blk")
    return jax.shard_map(
        on_device, mesh=mesh, in_specs=in_specs, out_specs=out_specs, check_vma=False
    )
```

profile of v0, /device:TPU:1, one launch (start us, length us, event | category | flops | bytes accessed | tf_op | source)
XLA Modules:
  0.0 703.4 jit_solution(5454243177161245767)
XLA Ops:
  4.9 14.9 %all-to-all-start = ((s32[128,1,8]{2,1,0:T(1,128)}), s32[128,1,8]{2,1,0:T(1,128)S(1)}, u32[]{:S(2)}, u32[]{:S(2)}) async-start(s32[128,1,8]{2,1,0:T(1,128)} %bitcast.14), calls=%async_computation | async-start | bytes 131072 | tf_op jit(solution)/shard_map/all_to_all | solution.py:120
  22.8 160.4 %all_gather.7 = f32[7,32768]{1,0:T(8,128)S(1)} all-gather(f32[7,256]{1,0:T(8,128)S(1)} %concatenate.3), channel_id=1, replica_groups=mesh['blk'=128,'rhs'=2] {'blk'}, dimensions={1}, use_global_device_ids=true | all-gather | bytes 924672 | tf_op jit(solution)/shard_map/all_gather | solution.py:103
  183.2 151.7 %all-gather = f32[1,2,32768]{2,1,0:T(2,128)S(1)} all-gather(f32[1,2,256]{2,1,0:T(2,128)S(1)} %copy-done.2), channel_id=2, replica_groups=mesh['blk'=128,'rhs'=2] {'blk'}, dimensions={2}, use_global_device_ids=true | all-gather | bytes 264192 | tf_op jit(solution)/shard_map/all_gather | solution.py:104
  334.9 313.9 %while.13 = (s32[]{:T(128)}, f32[1,256]{1,0:T(1,128)S(1)}, f32[1,256]{1,0:T(1,128)S(1)}, f32[64,1,2,512]{3,2,1,0:T(2,128)S(1)}, f32[64,7,512]{2,1,0:T(8,128)S(1)...) while((s32[]{:T(128)}, f32[1,256]{1,0:T(1,128)S(1)}, f32[1,256]{1,0:T(1,128)S(1)}, ...), condition=%wide.region_3.4_spmd.clone, body=%wide.region_0.3_spmd.clone.sunk | while | flops 10487301 | bytes 5321883 | solution.py:72
  335.3 2.4 subtract_multiply_fusion.4
  340.2 2.4 subtract_multiply_fusion.4
  345.1 2.4 subtract_multiply_fusion.4
  350.0 2.4 subtract_multiply_fusion.4
  354.9 2.4 subtract_multiply_fusion.4
  359.8 2.4 subtract_multiply_fusion.4
  364.7 2.4 subtract_multiply_fusion.4
  369.6 2.4 subtract_multiply_fusion.4
  374.5 2.4 subtract_multiply_fusion.4
  384.4 2.4 subtract_multiply_fusion.4
  389.3 2.4 subtract_multiply_fusion.4
  394.2 2.4 subtract_multiply_fusion.4
  399.1 2.4 subtract_multiply_fusion.4
  404.0 2.4 subtract_multiply_fusion.4
  408.9 2.4 subtract_multiply_fusion.4
  413.8 2.4 subtract_multiply_fusion.4
  418.7 2.4 subtract_multiply_fusion.4
  423.6 2.4 subtract_multiply_fusion.4
  428.5 2.4 subtract_multiply_fusion.4
  433.4 2.4 subtract_multiply_fusion.4
  438.3 2.4 subtract_multiply_fusion.4
  443.2 2.4 subtract_multiply_fusion.4
  448.1 2.4 subtract_multiply_fusion.4
  453.0 2.4 subtract_multiply_fusion.4
  457.9 2.4 subtract_multiply_fusion.4
  462.8 2.4 subtract_multiply_fusion.4
  467.7 2.4 subtract_multiply_fusion.4
  477.6 2.4 subtract_multiply_fusion.4
  482.5 2.4 subtract_multiply_fusion.4
  487.4 2.4 subtract_multiply_fusion.4
  492.3 2.4 subtract_multiply_fusion.4
  497.2 2.4 subtract_multiply_fusion.4
  502.1 2.4 subtract_multiply_fusion.4
  507.0 2.4 subtract_multiply_fusion.4
  511.9 2.4 subtract_multiply_fusion.4
  516.8 2.4 subtract_multiply_fusion.4
  521.7 2.4 subtract_multiply_fusion.4
  526.6 2.4 subtract_multiply_fusion.4
  531.5 2.4 subtract_multiply_fusion.4
  649.2 2.8 gather_fusion
  653.4 5.3 all-to-all-start.1
  658.8 11.9 %all-to-all-done.1 = f32[1,2,128,8]{3,1,0,2:T(2,128)S(1)} async-done(((f32[1,2,128,8]{3,1,0,2:T(2,128)}), f32[1,2,128,8]{3,1,0,2:T(2,128)S(1)}, u32[]{:S(2)}, u32[]{:S(2)}) %all-to-all-start.1) | async-done | bytes 8224 | tf_op jit(solution)/shard_map/all_to_all | solution.py:122
  672.2 27.7 %gather_fusion.2 = f32[8192,2]{1,0:T(8,128)} fusion(f32[2,256]{0,1:T(8,128)S(1)} %bitcast.135, s32[8192]{0:T(1024)S(1)} %broadcast_clamp_fusion), kind=kCustom, calls=%fused_computation.2 | custom fusion | bytes 163840 | tf_op jit(solution)/shard_map/gather | solution.py:77
  699.9 2.9 copy.29
  (767 shorter events, 228.9 us)
Async XLA Ops:
  0.0 334.9 %copy-start = (f32[3,256]{1,0:T(4,128)S(1)}, f32[3,256]{1,0:T(4,128)}, u32[]{:S(2)}) copy-start(f32[3,256]{1,0:T(4,128)} %param.10) | copy-start | bytes 9220
  0.0 183.2 %copy-start.2 = (f32[1,2,256]{2,1,0:T(2,128)S(1)}, f32[1,2,256]{2,1,0:T(2,128)}, u32[]{:S(2)}) copy-start(f32[1,2,256]{2,1,0:T(2,128)} %param.13) | copy-start | bytes 6148
  4.9 644.1 %all-to-all-start = ((s32[128,1,8]{2,1,0:T(1,128)}), s32[128,1,8]{2,1,0:T(1,128)S(1)}, u32[]{:S(2)}, u32[]{:S(2)}) async-start(s32[128,1,8]{2,1,0:T(1,128)} %bitcast.14), calls=%async_computation | async-start | bytes 131072 | tf_op jit(solution)/shard_map/all_to_all | solution.py:120
  653.4 17.2 %all-to-all-start.1 = ((f32[1,2,128,8]{3,1,0,2:T(2,128)}), f32[1,2,128,8]{3,1,0,2:T(2,128)S(1)}, u32[]{:S(2)}, u32[]{:S(2)}) async-start(f32[1,2,128,8]{3,1,0,2:T(2,128)} %bitcast.18), calls=%async_computation.1 | async-start | bytes 262144 | tf_op jit(solution)/shard_map/all_to_all | solution.py:122
  699.9 2.9 copy-start.1
where the time goes:
time: 704 us; the launch traced here: 703 us
  blocking collectives  312 us (44%)
  other arithmetic  179 us (25%)
  matrix products  133 us (19%)
  local copies, waits for them, and re-layouts  42.6 us (6%)
  starting transfers between devices  20.2 us (3%)
  waiting for transfers between devices  11.9 us (2%)
    all_gather x1, blocking collectives, on_device(): lax.all_gather(geometry, 'blk', axis=1, tiled=True)  160 us
    mul x64, other arithmetic, kernel_tile(): weight * (double * (sines - phases * cosine) - COUPLE * single * cosine)  152 us
    all_gather x1, blocking collectives, on_device(): lax.all_gather(send_density, 'blk', axis=1, tiled=True)  152 us
    dot_general x64, matrix products, apply_tile(): jnp.einsum('ts,rs->rt', imag_part, src_imag, precision=highest)  33.7 us
    dot_general x64, matrix products, apply_tile(): jnp.einsum('ts,rs->rt', imag_part, src_real, precision=highest)  33.6 us
    dot_general x64, matrix products, apply_tile(): jnp.einsum('ts,rs->rt', real_part, src_real, precision=highest)  33.6 us
    dot_general x64, matrix products, apply_tile(): jnp.einsum('ts,rs->rt', real_part, src_imag, precision=highest)  32.5 us
    gather x2, local copies, waits for them, and re-layouts, near_field(): looked = needed[:, :, near_rows]  30.6 us
  transfers between devices with their start and end apart: 2, of which 1 were waited for; matrix products, arithmetic and copies ran while one was open for 45% of the time, Pallas kernels for 0%

commit v1 on v0

--- a/solution.py
+++ b/solution.py
@@ -100,7 +100,9 @@
     far_real, far_imag = far_piece(
         (empty_sum, empty_sum),
         positions,
-        lax.all_gather(geometry, "blk", axis=1, tiled=True),
+        jnp.concatenate(
+            lax.all_to_all(jnp.stack([geometry] * lax.axis_size("blk")), "blk", 0, 0), axis=1
+        ),
         lax.all_gather(send_density, "blk", axis=1, tiled=True),
     )
     near_sides = densities.shape[0]

time: 704 us -> 578 us (0.82)
  blocking collectives: 312 us -> 171 us
  waiting for transfers between devices: 11.9 us -> 20.7 us
    all_gather x1 -> x0, blocking collectives: 160 us -> none  [on_device(): lax.all_gather(geometry, 'blk', axis=1, tiled=True)]
    all_gather x1, blocking collectives: 152 us -> 171 us  [on_device(): lax.all_gather(send_density, 'blk', axis=1, tiled=True)]
    all_to_all x1, waiting for transfers between devices: 0.01 us -> 8.91 us  [on_device(): lax.all_to_all(requests, 'blk', split_axis=0, concat_axis=0, tiled=True)]
  transfers between devices with their start and end apart: 2 -> 3, of which waited for: 1 -> 2; matrix products, arithmetic and copies ran while one was open for 45% -> 6% of each run, Pallas kernels for 0% -> 0%
where the time goes in v1:
time: 578 us; the launch traced here: 577 us
  other arithmetic  178 us (31%)
  blocking collectives  171 us (30%)
  matrix products  133 us (23%)
  local copies, waits for them, and re-layouts  43.6 us (8%)
  starting transfers between devices  26.2 us (5%)
  waiting for transfers between devices  20.7 us (4%)
    all_gather x1, blocking collectives, on_device(): lax.all_gather(send_density, 'blk', axis=1, tiled=True)  171 us
    mul x64, other arithmetic, kernel_tile(): weight * (double * (sines - phases * cosine) - COUPLE * single * cosine)  152 us
    dot_general x64, matrix products, apply_tile(): jnp.einsum('ts,rs->rt', imag_part, src_imag, precision=highest)  33.7 us
    dot_general x64, matrix products, apply_tile(): jnp.einsum('ts,rs->rt', imag_part, src_real, precision=highest)  33.6 us
    dot_general x64, matrix products, apply_tile(): jnp.einsum('ts,rs->rt', real_part, src_real, precision=highest)  33.6 us
    dot_general x64, matrix products, apply_tile(): jnp.einsum('ts,rs->rt', real_part, src_imag, precision=highest)  32.5 us
    gather x2, local copies, waits for them, and re-layouts, near_field(): looked = needed[:, :, near_rows]  30.6 us
    reduce_sum x64, other arithmetic, kernel_tile(): facing = jnp.sum(offset_vec * geometry[3:6, None, :], 0)  19.8 us
  transfers between devices with their start and end apart: 3, of which 2 were waited for; matrix products, arithmetic and copies ran while one was open for 6% of the time, Pallas kernels for 0%

profile of v1, /device:TPU:1, one launch (start us, length us, event | category | flops | bytes accessed | tf_op | source)
XLA Modules:
  0.0 576.7 jit_solution(6609428031072205278)
XLA Ops:
  4.9 14.9 %all-to-all-start.1 = ((s32[128,1,8]{2,1,0:T(1,128)}), s32[128,1,8]{2,1,0:T(1,128)S(1)}, u32[]{:S(2)}, u32[]{:S(2)}) async-start(s32[128,1,8]{2,1,0:T(1,128)} %bitcast.15), calls=%async_computation.1 | async-start | bytes 131072 | tf_op jit(solution)/shard_map/all_to_all | solution.py:122
  21.5 8.9 %all-to-all-done.1 = s32[128,1,8]{2,1,0:T(1,128)S(1)} async-done(((s32[128,1,8]{2,1,0:T(1,128)}), s32[128,1,8]{2,1,0:T(1,128)S(1)}, u32[]{:S(2)}, u32[]{:S(2)}) %all-to-all-start.1) | async-done | bytes 4128 | tf_op jit(solution)/shard_map/all_to_all | solution.py:122
  30.5 2.8 gather_fusion
  34.8 5.8 %all-to-all-start.2 = ((f32[1,2,128,8]{3,1,0,2:T(2,128)}), f32[1,2,128,8]{3,1,0,2:T(2,128)S(1)}, u32[]{:S(2)}, u32[]{:S(2)}) async-start(f32[1,2,128,8]{3,1,0,2:T(2,128)} %bitcast.19), calls=%async_computation.2 | async-start | bytes 262144 | tf_op jit(solution)/shard_map/all_to_all | solution.py:124
  40.6 11.8 %all-to-all-done.2 = f32[1,2,128,8]{3,1,0,2:T(2,128)S(1)} async-done(((f32[1,2,128,8]{3,1,0,2:T(2,128)}), f32[1,2,128,8]{3,1,0,2:T(2,128)S(1)}, u32[]{:S(2)}, u32[]{:S(2)}) %all-to-all-start.2) | async-done | bytes 8224 | tf_op jit(solution)/shard_map/all_to_all | solution.py:124
  53.5 5.6 all-to-all-start
  59.2 170.8 %all-gather = f32[1,2,32768]{2,1,0:T(2,128)S(1)} all-gather(f32[1,2,256]{2,1,0:T(2,128)S(1)} %copy-done.3), channel_id=2, replica_groups=mesh['blk'=128,'rhs'=2] {'blk'}, dimensions={2}, use_global_device_ids=true | all-gather | bytes 264192 | tf_op jit(solution)/shard_map/all_gather | solution.py:106
  231.5 27.7 %gather_fusion.2 = f32[8192,2]{1,0:T(8,128)} fusion(f32[2,256]{0,1:T(8,128)S(1)} %bitcast.137, s32[8192]{0:T(1024)S(1)} %broadcast_clamp_fusion), kind=kCustom, calls=%fused_computation.2 | custom fusion | bytes 163840 | tf_op jit(solution)/shard_map/gather | solution.py:77
  259.2 2.9 copy.29
  262.1 313.9 %while.13 = (s32[]{:T(128)}, f32[1,256]{1,0:T(1,128)S(1)}, f32[1,256]{1,0:T(1,128)S(1)}, f32[64,1,2,512]{3,2,1,0:T(2,128)S(1)}, f32[64,7,512]{2,1,0:T(8,128)S(1)...) while((s32[]{:T(128)}, f32[1,256]{1,0:T(1,128)S(1)}, f32[1,256]{1,0:T(1,128)S(1)}, ...), condition=%wide.region_3.4_spmd.clone, body=%wide.region_0.3_spmd.clone.sunk | while | flops 10487301 | bytes 5321883 | solution.py:72
  262.5 2.4 subtract_multiply_fusion.4
  267.4 2.4 subtract_multiply_fusion.4
  272.3 2.4 subtract_multiply_fusion.4
  277.2 2.4 subtract_multiply_fusion.4
  282.1 2.4 subtract_multiply_fusion.4
  287.0 2.4 subtract_multiply_fusion.4
  296.8 2.4 subtract_multiply_fusion.4
  301.8 2.4 subtract_multiply_fusion.4
  306.7 2.4 subtract_multiply_fusion.4
  311.6 2.4 subtract_multiply_fusion.4
  316.5 2.4 subtract_multiply_fusion.4
  321.4 2.4 subtract_multiply_fusion.4
  326.3 2.4 subtract_multiply_fusion.4
  331.2 2.4 subtract_multiply_fusion.4
  336.1 2.4 subtract_multiply_fusion.4
  341.0 2.4 subtract_multiply_fusion.4
  345.9 2.4 subtract_multiply_fusion.4
  350.8 2.4 subtract_multiply_fusion.4
  355.7 2.4 subtract_multiply_fusion.4
  360.6 2.4 subtract_multiply_fusion.4
  365.5 2.4 subtract_multiply_fusion.4
  370.4 2.4 subtract_multiply_fusion.4
  375.3 2.4 subtract_multiply_fusion.4
  380.2 2.4 subtract_multiply_fusion.4
  390.0 2.4 subtract_multiply_fusion.4
  395.0 2.4 subtract_multiply_fusion.4
  399.9 2.4 subtract_multiply_fusion.4
  404.8 2.4 subtract_multiply_fusion.4
  409.7 2.4 subtract_multiply_fusion.4
  414.6 2.4 subtract_multiply_fusion.4
  419.5 2.4 subtract_multiply_fusion.4
  424.4 2.4 subtract_multiply_fusion.4
  429.3 2.4 subtract_multiply_fusion.4
  434.2 2.4 subtract_multiply_fusion.4
  439.1 2.4 subtract_multiply_fusion.4
  444.0 2.4 subtract_multiply_fusion.4
  448.9 2.4 subtract_multiply_fusion.4
  453.8 2.4 subtract_multiply_fusion.4
  (773 shorter events, 230.9 us)
Async XLA Ops:
  1.1 39.5 %copy-start.4 = (f32[256]{0:T(256)S(1)}, f32[256]{0:T(256)}, u32[]{:S(2)}) copy-start(f32[256]{0:T(256)} %param.12) | copy-start | bytes 3076
  1.1 39.5 %copy-start = (f32[3,256]{1,0:T(4,128)S(1)}, f32[3,256]{1,0:T(4,128)}, u32[]{:S(2)}) copy-start(f32[3,256]{1,0:T(4,128)} %param.10) | copy-start | bytes 9220
  4.9 25.4 %all-to-all-start.1 = ((s32[128,1,8]{2,1,0:T(1,128)}), s32[128,1,8]{2,1,0:T(1,128)S(1)}, u32[]{:S(2)}, u32[]{:S(2)}) async-start(s32[128,1,8]{2,1,0:T(1,128)} %bitcast.15), calls=%async_computation.1 | async-start | bytes 131072 | tf_op jit(solution)/shard_map/all_to_all | solution.py:122
  34.8 17.7 %all-to-all-start.2 = ((f32[1,2,128,8]{3,1,0,2:T(2,128)}), f32[1,2,128,8]{3,1,0,2:T(2,128)S(1)}, u32[]{:S(2)}, u32[]{:S(2)}) async-start(f32[1,2,128,8]{3,1,0,2:T(2,128)} %bitcast.19), calls=%async_computation.2 | async-start | bytes 262144 | tf_op jit(solution)/shard_map/all_to_all | solution.py:124
  40.6 18.5 %copy-start.2 = (s32[32,256]{1,0:T(8,128)S(1)}, s32[32,256]{1,0:T(8,128)}, u32[]{:S(2)}) copy-start(s32[32,256]{1,0:T(8,128)} %param.16) | copy-start | bytes 98308
  40.6 18.5 %copy-start.3 = (f32[1,2,256]{2,1,0:T(2,128)S(1)}, f32[1,2,256]{2,1,0:T(2,128)}, u32[]{:S(2)}) copy-start(f32[1,2,256]{2,1,0:T(2,128)} %param.13) | copy-start | bytes 6148
  53.5 208.7 %all-to-all-start = ((f32[128,7,256]{2,1,0:T(8,128)}), f32[128,7,256]{2,1,0:T(8,128)S(1)}, u32[]{:S(2)}, u32[]{:S(2)}) async-start(f32[128,7,256]{2,1,0:T(8,128)} %stack.8), calls=%async_computation | async-start | bytes 2097152 | tf_op jit(solution)/shard_map/all_to_all | solution.py:104
  259.2 2.9 copy-start.1
